TPU v7x, 32 devices: a whole 2x2x4 slice. The times are simulated.
32 devices in a mesh: batch: 4 (over z), seq: 2 (over core), ch: 4 (over y, x).
Axes of the slice: x: 2, y: 2, z: 4, core: 2. Of those that a mesh axis runs over, the one named last changes fastest.
Arguments:
- inputs: bfloat16 [16, 1280, 2048], P('batch', 'ch', 'seq'), may hold values from -6 to 6
- segment_ids: int32 [16, 2048], P('batch', 'seq'), may hold values from 0 to 7, never falling along the last dimension, each value on 1 to 512 neighbouring positions
- norm0_gain: float32 [1280], P('ch'), may hold values from 0.1 to 1.9
- norm0_shift: float32 [1280], P('ch'), may hold values from -3 to 3
- w_inner: bfloat16 [1280, 640], P('ch'), may hold values from -0.15625 to 0.15625
- b_inner: float32 [640], P('ch'), may hold values from -3 to 3
- norm1_gain: float32 [640], P('ch'), may hold values from 0.1 to 1.9
- norm1_shift: float32 [640], P('ch'), may hold values from -3 to 3
- w_conv: bfloat16 [5, 640, 640], P(None, 'ch'), may hold values from -0.109375 to 0.109375
- b_conv: float32 [640], P('ch'), may hold values from -3 to 3
- norm2_gain: float32 [640], P('ch'), may hold values from 0.1 to 1.9
- norm2_shift: float32 [640], P('ch'), may hold values from -3 to 3
- w_outer: bfloat16 [640, 1280], P('ch'), may hold values from -0.25 to 0.25
- b_outer: float32 [1280], P('ch'), may hold values from -3 to 3
- cotangent: bfloat16 [16, 1280, 2048], P('batch', 'ch', 'seq'), may hold values from -6 to 6
Outputs:
- output: bfloat16 [16, 1280, 2048], P('batch', 'ch', 'seq')
- input_grad: bfloat16 [16, 1280, 2048], P('batch', 'ch', 'seq')
- grad_norm0_gain: float32 [1280], P('ch')
- grad_norm0_shift: float32 [1280], P('ch')
- grad_w_inner: float32 [1280, 640], P('ch')
- grad_b_inner: float32 [640], P('ch')
- grad_norm1_gain: float32 [640], P('ch')
- grad_norm1_shift: float32 [640], P('ch')
- grad_w_conv: float32 [5, 640, 640], P(None, 'ch')
- grad_b_conv: float32 [640], P('ch')
- grad_norm2_gain: float32 [640], P('ch')
- grad_norm2_shift: float32 [640], P('ch')
- grad_w_outer: float32 [640, 1280], P('ch')
- grad_b_outer: float32 [1280], P('ch')
Inputs may be any that keep to these rules, and one draw needn't show every extreme that they name: `segment_ids`: along a row the ids never fall; each protein is one run of 1 to 512 residues, one run of each row has exactly 512, and every row holds all 8 ids.
All inputs are finite; a program needn't handle non-finite values.
Results may differ from a plain program's by a relative error of at most 0.0065.
Values may be sent and summed in bfloat16 or wider, within the bound.
A program may use at most 192 MiB of HBM per device.

v0:
```python
import functools
import math

import jax
import jax.numpy as jnp
from jax import lax
from jax.experimental import pallas as pl
from jax.experimental.pallas import tpu as pltpu
from jax.sharding import PartitionSpec as P

KERNEL_TAPS = 5
DILATION_SPACING = 32


EPSILON = 1e-05


MESH_AXES = ("batch", "seq", "ch")
MESH_ID = pl.DeviceIdType.MESH


def _exchange_kernel(sizes, group, gather, x_ref, o_ref, send_sem, recv_sem, own_sem):
    coords = {a: lax.axis_index(a) for a in MESH_AXES}
    me = 0
    for a in group:
        me = me * sizes[a] + coords[a]
    count = math.prod(sizes[a] for a in group)

    def device(index):
        where = dict(coords)
        rest = index
        for a in reversed(group):
            where[a] = lax.rem(rest, sizes[a])
            rest = rest // sizes[a]
        return tuple(where[a] for a in MESH_AXES)

    barrier = pltpu.get_barrier_semaphore()
    for j in range(1, count):
        pl.semaphore_signal(barrier, 1, device_id=device(lax.rem(me + j, count)), device_id_type=MESH_ID)
    pl.semaphore_wait(barrier, count - 1)
    copies = []
    for j in range(1, count):
        peer = lax.rem(me + j, count)
        copy = pltpu.make_async_remote_copy(
            src_ref=x_ref if gather else x_ref.at[peer],
            dst_ref=o_ref.at[me],
            send_sem=send_sem.at[j - 1],
            recv_sem=recv_sem.at[j - 1],
            device_id=device(peer),
            device_id_type=MESH_ID,
        )
        copy.start()
        copies.append(copy)
    own = pltpu.make_async_copy(x_ref if gather else x_ref.at[me], o_ref.at[me], own_sem)
    own.start()
    own.wait()
    for copy in copies:
        copy.wait()


def exchange(x, group, collective_id, gather=False):
    sizes = {a: lax.axis_size(a) for a in MESH_AXES}
    count = math.prod(sizes[a] for a in group)
    if count == 1:
        return x[None] if gather else x
    out_shape = (count,) + x.shape if gather else x.shape
    moved = x.size * x.dtype.itemsize * (count if gather else 1)
    return pl.pallas_call(
        functools.partial(_exchange_kernel, sizes, group, gather),
        out_shape=jax.ShapeDtypeStruct(out_shape, x.dtype),
        in_specs=[pl.BlockSpec(memory_space=pl.ANY)],
        out_specs=pl.BlockSpec(memory_space=pl.ANY),
        scratch_shapes=[
            pltpu.SemaphoreType.DMA((count - 1,)),
            pltpu.SemaphoreType.DMA((count - 1,)),
            pltpu.SemaphoreType.DMA(()),
        ],
        compiler_params=pltpu.CompilerParams(collective_id=collective_id, has_side_effects=True),
        cost_estimate=pl.CostEstimate(flops=0, transcendentals=0, bytes_accessed=2 * moved),
    )(x)


def gelu_exact(values):
    return jax.nn.gelu(values, approximate=False)


def gelu_back(point, grad):
    return jax.vjp(gelu_exact, point)[1](grad)[0]


def normalize(values, gain, shift):
    center = jnp.mean(values, axis=1, keepdims=True)
    offset = values - center
    spread = jnp.mean(offset * offset, axis=1, keepdims=True)
    scale = lax.rsqrt(spread + EPSILON)
    unit = offset * scale
    return (unit * gain[:, None] + shift[:, None], unit, scale)


def normalize_back(grad, unit, scale, gain):
    scaled = grad * gain[:, None]
    first = jnp.mean(scaled, axis=1, keepdims=True)
    second = jnp.mean(scaled * unit, axis=1, keepdims=True)
    return scale * (scaled - first - unit * second)


def neighbour_pairs(seqs, nch, q_count):
    pairs = []
    for s in range(seqs):
        for c in range(nch):
            q = c % q_count
            if q < q_count - 1:
                pairs.append((s * nch + c, s * nch + c + 1))
            elif s < seqs - 1:
                pairs.append((s * nch + c, (s + 1) * nch + c - (q_count - 1)))
    return pairs


def extended(x, width, pairs):
    down = [(j, i) for i, j in pairs]
    length = x.shape[-1]
    before = lax.ppermute(x[..., length - width :], ("seq", "ch"), pairs)
    after = lax.ppermute(x[..., :width], ("seq", "ch"), down)
    return jnp.concatenate([before, x, after], axis=-1)


def shifted_taps(wide, wide_ids, own_ids, offsets, border):
    length = own_ids.shape[-1]
    pieces = []
    for offset in offsets:
        lower = border + offset
        shifted = wide[:, :, lower : lower + length]
        matching = wide_ids[:, lower : lower + length] == own_ids
        pieces.append(jnp.where(matching[:, None, :], shifted, jnp.zeros_like(shifted)))
    return jnp.concatenate(pieces, axis=1)


def to_positions(x, nch, q_count):
    rows, width, length = x.shape
    if q_count > 1:
        x = x.reshape(rows, width, q_count, length // q_count).transpose(0, 2, 1, 3)
        x = x.reshape(rows * q_count, width, length // q_count)
    x = lax.all_to_all(x, "ch", 0, 0, tiled=True)
    return _join(x, nch)


def _join(x, nch):
    total, width, length = x.shape
    p = total // nch
    return x.reshape(nch, p, width, length).transpose(1, 0, 2, 3).reshape(p, nch * width, length)


def to_channels(x, nch, q_count, rows):
    p, width, length = x.shape
    x = x.reshape(p, nch, width // nch, length).transpose(1, 0, 2, 3).reshape(nch * p, width // nch, length)
    x = lax.all_to_all(x, "ch", 0, 0, tiled=True)
    if q_count > 1:
        _, width, part = x.shape
        x = x.reshape(rows, q_count, width, part).transpose(0, 2, 1, 3).reshape(rows, width, q_count * part)
    return x


def local(
    inputs,
    segment_ids,
    norm0_gain,
    norm0_shift,
    w_inner,
    b_inner,
    norm1_gain,
    norm1_shift,
    w_conv,
    b_conv,
    norm2_gain,
    norm2_shift,
    w_outer,
    b_outer,
    cotangent,
):
    nch = lax.axis_size("ch")
    seqs = lax.axis_size("seq")
    batches = lax.axis_size("batch")
    rows, dloc, length = inputs.shape
    hloc = w_conv.shape[1]
    hid = hloc * nch
    dim = dloc * nch
    if rows % nch == 0:
        q_count = 1
    else:
        q_count = nch // rows
    part = length // q_count
    border = 2 * DILATION_SPACING
    offsets = [(k - KERNEL_TAPS // 2) * DILATION_SPACING for k in range(KERNEL_TAPS)]
    back_offsets = [-o for o in offsets]
    pairs = neighbour_pairs(seqs, nch, q_count)
    me = lax.axis_index("ch")

    smalls = [norm0_gain, norm0_shift, b_inner, norm1_gain, norm1_shift, b_conv, norm2_gain, norm2_shift, b_outer]
    small_all = exchange(jnp.concatenate(smalls), ("ch",), 0, gather=True)
    cut = 0
    full = []
    for v in smalls:
        n = v.shape[0]
        full.append(small_all[:, cut : cut + n].reshape(n * nch))
        cut += n
    g0, s0, b_in, g1, s1, b_cv, g2, s2, b_out = full
    sidx = lax.axis_index("seq")
    w_in = lax.dynamic_slice_in_dim(w_inner, sidx * (dloc // seqs), dloc // seqs, 0)
    w_cv = lax.dynamic_slice_in_dim(w_conv, sidx * (hloc // seqs), hloc // seqs, 1)
    w_out = lax.dynamic_slice_in_dim(w_outer, sidx * (hloc // seqs), hloc // seqs, 0)
    w_in = exchange(exchange(w_in, ("ch",), 1, gather=True), ("seq",), 2, gather=True)
    w_cv = exchange(exchange(w_cv, ("ch",), 3, gather=True), ("seq",), 4, gather=True)
    w_out = exchange(exchange(w_out, ("ch",), 5, gather=True), ("seq",), 6, gather=True)
    w_in = w_in.transpose(1, 0, 2, 3).reshape(dim, hid)
    w_cv = w_cv.transpose(2, 1, 0, 3, 4).reshape(KERNEL_TAPS, hid, hid)
    w_out = w_out.transpose(1, 0, 2, 3).reshape(hid, dim)

    x = to_positions(inputs, nch, q_count)
    cot = to_positions(cotangent, nch, q_count)
    prow = x.shape[0]
    if q_count == 1:
        ids = lax.dynamic_slice_in_dim(segment_ids, me * prow, prow, axis=0)
    else:
        ids = lax.dynamic_slice_in_dim(segment_ids, me // q_count, 1, axis=0)
        ids = lax.dynamic_slice_in_dim(ids, (me % q_count) * part, part, axis=1)
    own_ids = ids + 1
    wide_ids = extended(own_ids, border, pairs)

    residual = x.astype(jnp.float32)
    normed0, unit0, scale0 = normalize(residual, g0, s0)
    hidden0 = gelu_exact(normed0).astype(jnp.bfloat16)
    inner = jnp.einsum("dh,rdl->rhl", w_in, hidden0, preferred_element_type=jnp.float32) + b_in[:, None]
    normed1, unit1, scale1 = normalize(inner, g1, s1)
    hidden1 = gelu_exact(normed1).astype(jnp.bfloat16)
    wide_hidden = extended(hidden1, border, pairs)
    taps = shifted_taps(wide_hidden, wide_ids, own_ids, offsets, border)
    kernel_flat = w_cv.reshape(KERNEL_TAPS * hid, hid)
    mixed = jnp.einsum("co,rcl->rol", kernel_flat, taps, preferred_element_type=jnp.float32) + b_cv[:, None]
    normed2, unit2, scale2 = normalize(mixed, g2, s2)
    hidden2 = gelu_exact(normed2).astype(jnp.bfloat16)
    branch = jnp.einsum("hd,rhl->rdl", w_out, hidden2, preferred_element_type=jnp.float32)
    output = (residual + branch + b_out[:, None]).astype(jnp.bfloat16)

    grad_b_outer = jnp.sum(cot.astype(jnp.float32), axis=(0, 2))
    grad_w_outer = jnp.einsum("rhl,rdl->hd", hidden2, cot, preferred_element_type=jnp.float32)
    grad_hidden2 = jnp.einsum("hd,rdl->rhl", w_out, cot, preferred_element_type=jnp.float32)
    grad_normed2 = gelu_back(normed2, grad_hidden2)
    grad_norm2_gain = jnp.sum(grad_normed2 * unit2, axis=(0, 2))
    grad_norm2_shift = jnp.sum(grad_normed2, axis=(0, 2))
    grad_mixed = normalize_back(grad_normed2, unit2, scale2, g2).astype(jnp.bfloat16)
    grad_b_conv = jnp.sum(grad_mixed.astype(jnp.float32), axis=(0, 2))
    grad_w_conv = jnp.einsum(
        "rkcil,rol->ckio",
        taps.reshape(prow, KERNEL_TAPS, nch, hloc, part),
        grad_mixed,
        preferred_element_type=jnp.float32,
    )
    wide_grad = extended(grad_mixed, border, pairs)
    back_taps = shifted_taps(wide_grad, wide_ids, own_ids, back_offsets, border)
    kernel_back = jnp.transpose(w_cv, (0, 2, 1)).reshape(KERNEL_TAPS * hid, hid)
    grad_hidden1 = jnp.einsum("oc,rol->rcl", kernel_back, back_taps, preferred_element_type=jnp.float32)
    grad_normed1 = gelu_back(normed1, grad_hidden1)
    grad_norm1_gain = jnp.sum(grad_normed1 * unit1, axis=(0, 2))
    grad_norm1_shift = jnp.sum(grad_normed1, axis=(0, 2))
    grad_inner = normalize_back(grad_normed1, unit1, scale1, g1).astype(jnp.bfloat16)
    grad_b_inner = jnp.sum(grad_inner.astype(jnp.float32), axis=(0, 2))
    grad_w_inner = jnp.einsum("rdl,rhl->dh", hidden0, grad_inner, preferred_element_type=jnp.float32)
    grad_hidden0 = jnp.einsum("dh,rhl->rdl", w_in, grad_inner, preferred_element_type=jnp.float32)
    grad_normed0 = gelu_back(normed0, grad_hidden0)
    grad_norm0_gain = jnp.sum(grad_normed0 * unit0, axis=(0, 2))
    grad_norm0_shift = jnp.sum(grad_normed0, axis=(0, 2))
    input_grad = (cot.astype(jnp.float32) + normalize_back(grad_normed0, unit0, scale0, g0)).astype(jnp.bfloat16)

    output = to_channels(output, nch, q_count, rows)
    input_grad = to_channels(input_grad, nch, q_count, rows)

    vectors = [
        grad_norm0_gain,
        grad_norm0_shift,
        grad_b_inner,
        grad_norm1_gain,
        grad_norm1_shift,
        grad_b_conv,
        grad_norm2_gain,
        grad_norm2_shift,
        grad_b_outer,
    ]
    flat = jnp.concatenate([v.reshape(nch, -1) for v in vectors], axis=1)
    vec_len = flat.shape[1]
    vec_rows = -(-vec_len // dim)
    flat = jnp.pad(flat, ((0, 0), (0, vec_rows * dim - vec_len))).reshape(nch, vec_rows, dim)
    outer_plus = jnp.concatenate([grad_w_outer.reshape(nch, hloc, dim), flat], axis=1)

    def reduce_weight(g, split_dim, cid):
        g = lax.psum_scatter(g, "seq", scatter_dimension=split_dim, tiled=True)
        g = lax.psum_scatter(g, "batch", scatter_dimension=split_dim, tiled=True)
        g = jnp.sum(exchange(g, ("ch",), cid), axis=0)
        g = exchange(g, ("seq", "batch"), cid + 1, gather=True)
        return jnp.moveaxis(g, 0, split_dim - 1)

    red_outer = reduce_weight(outer_plus, 2, 7)
    red_outer = red_outer.reshape(hloc + vec_rows, dim)
    red_w_outer = red_outer[:hloc]
    mine = red_outer[hloc:].reshape(-1)[:vec_len]
    red_w_conv = reduce_weight(grad_w_conv, 3, 9)
    red_w_conv = red_w_conv.reshape(KERNEL_TAPS, hloc, hid)
    red_w_inner = reduce_weight(grad_w_inner.reshape(nch, dloc, hid), 1, 11).reshape(dloc, hid)
    reds = []
    cut = 0
    for v in vectors:
        n = v.shape[0] // nch
        reds.append(mine[cut : cut + n])
        cut += n
    return (
        output,
        input_grad,
        reds[0],
        reds[1],
        red_w_inner,
        reds[2],
        reds[3],
        reds[4],
        red_w_conv,
        reds[5],
        reds[6],
        reds[7],
        red_w_outer,
        reds[8],
    )


def solution(mesh):
    return jax.shard_map(
        local,
        mesh=mesh,
        in_specs=(
            P("batch", "ch", "seq"),
            P("batch", "seq"),
            P("ch"),
            P("ch"),
            P("ch", None),
            P("ch"),
            P("ch"),
            P("ch"),
            P(None, "ch", None),
            P("ch"),
            P("ch"),
            P("ch"),
            P("ch", None),
            P("ch"),
            P("batch", "ch", "seq"),
        ),
        out_specs=(
            P("batch", "ch", "seq"),
            P("batch", "ch", "seq"),
            P("ch"),
            P("ch"),
            P("ch", None),
            P("ch"),
            P("ch"),
            P("ch"),
            P(None, "ch", None),
            P("ch"),
            P("ch"),
            P("ch"),
            P("ch", None),
            P("ch"),
        ),
        check_vma=False,
    )
```

profile of v0, /device:TPU:0, one launch (start us, length us, event | category | flops | bytes accessed | tf_op | source)
XLA Modules:
  0.0 844.1 jit_solution(17330687690477803513)
XLA Ops:
  7.2 5.3 all-to-all-start
  18.4 34.5 %shard_map.259.x_ref = bf16[4,80,1280]{2,1,0:T(8,128)(2,1)} custom-call(bf16[80,1280]{1,0:T(8,128)(2,1)} %constant_dynamic-slice_fusion.x_ref), custom_call_target="tpu_custom_call" | custom-call | bytes 1638400 | tf_op jit(solution)/shard_map/pallas_call | solution.py:68
  53.0 26.0 %shard_map.260 = bf16[2,4,80,1280]{3,2,1,0:T(8,128)(2,1)} custom-call(bf16[4,80,1280]{2,1,0:T(8,128)(2,1)} %shard_map.259.x_ref), custom_call_target="tpu_custom_call" | custom-call | bytes 3276800 | tf_op jit(solution)/shard_map/pallas_call | solution.py:68
  82.4 5.0 shard_map.254
  89.3 25.2 %shard_map.257.x_ref = bf16[4,5,80,640]{3,2,1,0:T(8,128)(2,1)} custom-call(bf16[5,80,640]{2,1,0:T(8,128)(2,1)} %constant_dynamic-slice_fusion.1.x_ref), custom_call_target="tpu_custom_call" | custom-call | bytes 4096000 | tf_op jit(solution)/shard_map/pallas_call | solution.py:68
  114.4 63.2 %shard_map.258 = bf16[2,4,5,80,640]{4,3,2,1,0:T(8,128)(2,1)} custom-call(bf16[4,5,80,640]{3,2,1,0:T(8,128)(2,1)} %shard_map.257.x_ref), custom_call_target="tpu_custom_call" | custom-call | bytes 8192000 | tf_op jit(solution)/shard_map/pallas_call | solution.py:68
  177.7 4.7 copy.59
  183.3 13.1 %shard_map.255.x_ref = bf16[4,160,640]{2,1,0:T(8,128)(2,1)} custom-call(bf16[160,640]{1,0:T(8,128)(2,1)} %constant_dynamic-slice_fusion.2.x_ref), custom_call_target="tpu_custom_call" | custom-call | bytes 1638400 | tf_op jit(solution)/shard_map/pallas_call | solution.py:68
  196.4 26.0 %shard_map.256 = bf16[2,4,160,640]{3,2,1,0:T(8,128)(2,1)} custom-call(bf16[4,160,640]{2,1,0:T(8,128)(2,1)} %shard_map.255.x_ref), custom_call_target="tpu_custom_call" | custom-call | bytes 3276800 | tf_op jit(solution)/shard_map/pallas_call | solution.py:68
  225.1 7.8 copy.66
  233.1 4.6 all-to-all-start.2
  245.3 13.9 %fusion.88 = (f32[1024]{0:T(1024)S(1)}, f32[1024,640]{1,0:T(8,128)S(1)}) fusion(f32[640]{0:T(1024)S(1)} %add.171, bf16[1280,640]{1,0:T(8,128)(2,1)S(1)} %bitcast.277, f32[1280]{0:T(1024)S(1)} %add.167, f32[1280]{0:T(1024)S(1)} %mul.436, f32[1024]{0:T(1024)S(1)} %add_rsqrt_fusion.2, f32[1,1280,1,1,1,1,1024]{6,1,5,4,3,2,0:T(8,128)S(1)} %bitcast.259, ...), kind=kOutput, calls=%fused_computation.162 | convolution fusion | flops 1769470976 | bytes 9527808 | tf_op jit(solution)/shard_map/dh,rdl->rhl/dot_general | solution.py:232
  259.8 7.3 multiply_convert_fusion.1
  271.7 5.9 copy.61
  280.9 7.3 constant_dynamic-update-slice_fusion
  291.4 5.5 fusion.90
  298.3 11.5 %fusion.65 = (f32[640]{0:T(1024)S(1)}, f32[1024]{0:T(1024)S(1)}, f32[1024]{0:T(1024)S(1)}, f32[640]{0:T(1024)S(1)}, f32[1,640,1024]{1,2,0:T(8,128)S(1)}) fusion(f32[1024]{0:T(1024)S(1)} %add_rsqrt_fusion, f32[1024]{0:T(1024)S(1)} %broadcast_multiply_fusion.4, f32[640]{0:T(1024)S(1)} %add.179, f32[1024,640]{1,0:T(8,128)S(1)} %get-tuple-element.64, ...), kind=kOutput, calls=%fused_computation.113 | convolution fusion | flops 1732113152 | bytes 9531904 | tf_op jit(solution)/shard_map/hd,rdl->rhl/dot_general | solution.py:246
  309.8 8.1 convert_reduce_fusion.1
  325.1 5.8 fusion.190
  334.9 11.6 %fusion.71 = (f32[640]{0:T(1024)S(1)}, f32[1024]{0:T(1024)S(1)}, f32[1024]{0:T(1024)S(1)}, f32[640]{0:T(1024)S(1)}, f32[1,640,1024]{1,2,0:T(8,128)S(1)}) fusion(f32[1024]{0:T(1024)S(1)} %add_rsqrt_fusion.1, f32[1024]{0:T(1024)S(1)} %broadcast_multiply_fusion.5, f32[640]{0:T(1024)S(1)} %add.171, f32[1024,640]{1,0:T(8,128)S(1)} %copy-done.4, ...), kind=kOutput, calls=%fused_computation.124 | convolution fusion | flops 4248695808 | bytes 15921664 | tf_op jit(solution)/shard_map/oc,rol->rcl/dot_general | solution.py:261
  347.9 17.2 %multiply_reduce_fusion = (f32[1280]{0:T(1024)S(1)}, f32[1024]{0:T(1024)S(1)}, f32[1024]{0:T(1024)S(1)}, f32[1280]{0:T(1024)S(1)}, f32[1,1280,1024]{1,2,0:T(8,128)}) fusion(f32[1,1280,1024]{1,2,0:T(8,128)S(1)} %bitcast.258, f32[1024]{0:T(1024)S(1)} %broadcast_multiply_fusion.8, f32[1024]{0:T(1024)S(1)} %add_rsqrt_fusion.2, f32[1280]{0:T(1024)S(1)} %mul.436, ...), kind=kOutput, calls=%fused_computation.41 | convolution fusion | flops 1785196032 | bytes 13471744 | tf_op jit(solution)/shard_map/dh,rhl->rdl/dot_general | solution.py:268
  365.7 4.0 pad_maximum_fusion
  370.4 17.0 %fusion.84 = f32[4,320,640]{2,1,0:T(8,128)} fusion(bf16[4,320,1024]{2,1,0:T(8,128)(2,1)} %all-to-all-done, f32[4,320]{1,0:T(4,128)S(1)} %copy-done.22, f32[4,320]{1,0:T(4,128)S(1)} %copy-done.20, f32[1024]{0:T(1024)S(1)} %add_rsqrt_fusion.2, f32[1024]{0:T(1024)S(1)} %broadcast_multiply_fusion.8, bf16[1,640,1024]{1,2,0:T(8,128)(2,1)} %copy-done.14), kind=kOutput, calls=%fused_computation.158 | convolution fusion | flops 1769472000 | bytes 7227392 | tf_op jit(solution)/shard_map/rdl,rhl->dh/dot_general | solution.py:267
  387.5 9.9 %copy.74 = bf16[1,3200,1024]{2,1,0:T(8,128)(2,1)} copy(bf16[1,3200,1024]{1,2,0:T(8,128)(2,1)} %copy-done.7) | data formatting | bytes 13107200 | tf_op jit(solution)/shard_map/concatenate | solution.py:135
  397.3 10.2 %fusion.43 = f32[4,5,160,640]{3,2,1,0:T(8,128)} fusion(bf16[5,4,160,1024]{3,2,1,0:T(8,128)(2,1)} %bitcast.268, bf16[1,640,1024]{1,2,0:T(8,128)(2,1)S(1)} %get-tuple-element.33), kind=kOutput, calls=%fused_computation.85 | convolution fusion | flops 4194304000 | bytes 16056320 | tf_op jit(solution)/shard_map/rkcil,rol->ckio/dot_general | solution.py:252
  407.5 18.7 %copy.85 = f32[4,5,160,640]{2,1,0,3:T(8,128)} copy(f32[4,5,160,640]{3,2,1,0:T(8,128)} %fusion.43) | data formatting | bytes 16384000
  426.2 16.8 %reshape.1435 = f32[640,3200]{1,0:T(8,128)} reshape(f32[640,4,5,160]{3,2,1,0:T(8,128)} %bitcast.256) | data formatting | bytes 16384000
  443.1 3.8 copy.70
  447.6 13.8 %reduce-scatter.16.cloned.1.call-done = f32[320,3200]{1,0:T(8,128)} async-done(((f32[640,3200]{1,0:T(8,128)}), f32[320,3200]{1,0:T(8,128)}) %reduce-scatter.16.cloned.1.call-update) | async-done | bytes 4096016
  461.5 6.7 fusion.17
  468.3 4.4 copy.62
  472.7 4.6 all-to-all-start.1
  477.2 4.9 copy.67
  482.2 8.0 add_convert_fusion
  490.2 4.5 copy.68
  494.7 13.8 %all-to-all-done.1 = bf16[4,320,1024]{2,1,0:T(8,128)(2,1)} async-done(((bf16[4,320,1024]{2,1,0:T(8,128)(2,1)}), bf16[4,320,1024]{2,1,0:T(8,128)(2,1)}, u32[]{:S(2)}, u32[]{:S(2)}) %all-to-all-start.1) | async-done | bytes 2621472 | tf_op jit(solution)/shard_map/all_to_all | solution.py:156
  508.6 4.9 all-to-all-start.3
  514.7 29.3 %all-to-all-done.3 = bf16[4,320,1024]{2,1,0:T(8,128)(2,1)} async-done(((bf16[4,320,1024]{2,1,0:T(8,128)(2,1)}), bf16[4,320,1024]{2,1,0:T(8,128)(2,1)}, u32[]{:S(2)}, u32[]{:S(2)}) %all-to-all-start.3) | async-done | bytes 2621472 | tf_op jit(solution)/shard_map/all_to_all | solution.py:156
  544.0 25.0 %all-reduce.4.cloned.1.call-done = f32[4,162,640]{1,0,2:T(4,128)} async-done(((f32[4,162,640]{1,0,2:T(4,128)}), f32[4,162,640]{1,0,2:T(4,128)}) %all-reduce.4.cloned.1.call-update) | async-done | bytes 1658896
  571.4 11.1 %shard_map.261 = f32[4,162,160]{2,1,0:T(8,128)} custom-call(f32[4,162,160]{2,1,0:T(8,128)} %copy.71.x_ref), custom_call_target="tpu_custom_call" | custom-call | bytes 829440 | tf_op jit(solution)/shard_map/pallas_call | solution.py:68
  584.4 47.2 %shard_map.262 = f32[8,162,160]{2,1,0:T(8,128)} custom-call(f32[162,160]{1,0:T(8,128)} %reduce_sum.237.x_ref), custom_call_target="tpu_custom_call" | custom-call | bytes 1658880 | tf_op jit(solution)/shard_map/pallas_call | solution.py:68
  640.1 8.4 shard_map.263
  650.3 39.3 %shard_map.264 = f32[8,40,640]{2,1,0:T(8,128)} custom-call(f32[40,640]{1,0:T(8,128)} %reduce_sum.238.x_ref), custom_call_target="tpu_custom_call" | custom-call | bytes 1638400 | tf_op jit(solution)/shard_map/pallas_call | solution.py:68
  689.6 28.7 %reduce-scatter.18.cloned.1.call-done = f32[80,3200]{1,0:T(8,128)} async-done(((f32[320,3200]{1,0:T(8,128)}), f32[80,3200]{1,0:T(8,128)}) %reduce-scatter.18.cloned.1.call-update) | async-done | bytes 1024016
  724.7 21.4 %shard_map.265 = f32[4,5,160,80]{3,2,1,0:T(8,128)} custom-call(f32[4,5,160,80]{3,2,1,0:T(8,128)} %copy.88.x_ref), custom_call_target="tpu_custom_call" | custom-call | bytes 2048000 | tf_op jit(solution)/shard_map/pallas_call | solution.py:68
  748.4 70.8 %shard_map.266 = f32[8,5,160,80]{3,2,1,0:T(8,128)} custom-call(f32[5,160,80]{2,1,0:T(8,128)} %reduce_sum.239.x_ref), custom_call_target="tpu_custom_call" | custom-call | bytes 4096000 | tf_op jit(solution)/shard_map/pallas_call | solution.py:68
  819.2 5.5 copy.77
  824.7 4.3 reshape.1428
  (180 shorter events, 81.8 us)
Async XLA Ops:
  7.2 81.2 %copy-start = (bf16[5,160,640]{2,1,0:T(8,128)(2,1)S(1)}, bf16[5,160,640]{2,1,0:T(8,128)(2,1)}, u32[]{:S(2)}) copy-start(bf16[5,160,640]{2,1,0:T(8,128)(2,1)} %param.23) | copy-start | bytes 3072004
  7.2 10.4 %copy-start.16 = (bf16[160,1280]{1,0:T(8,128)(2,1)S(1)}, bf16[160,1280]{1,0:T(8,128)(2,1)}, u32[]{:S(2)}) copy-start(bf16[160,1280]{1,0:T(8,128)(2,1)} %param.27) | copy-start | bytes 1228804
  7.2 225.9 %all-to-all-start = ((bf16[4,320,1024]{2,1,0:T(8,128)(2,1)}), bf16[4,320,1024]{2,1,0:T(8,128)(2,1)}, u32[]{:S(2)}, u32[]{:S(2)}) async-start(bf16[4,320,1024]{2,1,0:T(8,128)(2,1)} %param.15), calls=%async_computation | async-start | bytes 5242880 | tf_op jit(solution)/shard_map/all_to_all | solution.py:143
  13.3 219.7 %collective-permute-start.2 = (s32[1,64]{1,0:T(1,128)S(1)}, s32[1,64]{1,0:T(1,128)S(1)}, u32[]{:S(2)}, u32[]{:S(2)}) collective-permute-start(s32[1,64]{1,0:T(1,128)S(1)} %get-tuple-element.60), channel_id=1, source_target_pairs={{4,0},{5,1},{6,2},{7,3},{12,8},{13,9},{14,10},{15,11},{20,16},{21,... | collective-permute-start | bytes 776 | tf_op jit(solution)/shard_map/ppermute | solution.py:123
  14.6 218.4 %collective-permute-start = (s32[1,64]{1,0:T(1,128)S(1)}, s32[1,64]{1,0:T(1,128)S(1)}, u32[]{:S(2)}, u32[]{:S(2)}) collective-permute-start(s32[1,64]{1,0:T(1,128)S(1)} %get-tuple-element.59), channel_id=1, source_target_pairs={{0,4},{1,5},{2,6},{3,7},{8,12},{9,13},{10,14},{11,15},{16,20},{17,... | collective-permute-start | bytes 776 | tf_op jit(solution)/shard_map/ppermute | solution.py:122
  52.8 28.8 %copy-start.23 = (f32[320]{0:T(512)S(1)}, f32[320]{0:T(512)}, u32[]{:S(2)}) copy-start(f32[320]{0:T(512)} %param.17) | copy-start | bytes 3844
  52.9 28.8 %copy-start.24 = (f32[320]{0:T(512)S(1)}, f32[320]{0:T(512)}, u32[]{:S(2)}) copy-start(f32[320]{0:T(512)} %param.18) | copy-start | bytes 3844
  52.9 28.8 %copy-start.25 = (f32[320]{0:T(512)S(1)}, f32[320]{0:T(512)}, u32[]{:S(2)}) copy-start(f32[320]{0:T(512)} %param.28) | copy-start | bytes 3844
  52.9 28.8 %copy-start.26 = (f32[160]{0:T(256)S(1)}, f32[160]{0:T(256)}, u32[]{:S(2)}) copy-start(f32[160]{0:T(256)} %param.20) | copy-start | bytes 1924
  52.9 28.8 %copy-start.27 = (f32[160]{0:T(256)S(1)}, f32[160]{0:T(256)}, u32[]{:S(2)}) copy-start(f32[160]{0:T(256)} %param.21) | copy-start | bytes 1924
  52.9 28.8 %copy-start.28 = (f32[160]{0:T(256)S(1)}, f32[160]{0:T(256)}, u32[]{:S(2)}) copy-start(f32[160]{0:T(256)} %param.22) | copy-start | bytes 1924
  52.9 28.8 %copy-start.29 = (f32[160]{0:T(256)S(1)}, f32[160]{0:T(256)}, u32[]{:S(2)}) copy-start(f32[160]{0:T(256)} %param.24) | copy-start | bytes 1924
  52.9 28.8 %copy-start.30 = (f32[160]{0:T(256)S(1)}, f32[160]{0:T(256)}, u32[]{:S(2)}) copy-start(f32[160]{0:T(256)} %param.25) | copy-start | bytes 1924
  52.9 28.8 %copy-start.31 = (f32[160]{0:T(256)S(1)}, f32[160]{0:T(256)}, u32[]{:S(2)}) copy-start(f32[160]{0:T(256)} %param.26) | copy-start | bytes 1924
  177.6 4.9 copy-start.17
  196.4 27.6 %copy-start.15 = (f32[4,1920]{1,0:T(4,128)S(1)}, f32[4,1920]{1,0:T(4,128)}, u32[]{:S(2)}) copy-start(f32[4,1920]{1,0:T(4,128)} %shard_map.254) | copy-start | bytes 92164
  224.0 21.3 %copy-start.12 = (bf16[4,2,160,640]{3,2,1,0:T(8,128)(2,1)}, bf16[4,2,160,640]{3,2,1,0:T(8,128)(2,1)S(1)}, u32[]{:S(2)}) copy-start(bf16[4,2,160,640]{3,2,1,0:T(8,128)(2,1)S(1)} %copy.58) | copy-start | bytes 4915204
  224.8 8.2 copy-start.19
  224.8 8.2 copy-start.21
  233.1 36.4 %all-to-all-start.2 = ((bf16[4,320,1024]{2,1,0:T(8,128)(2,1)}), bf16[4,320,1024]{2,1,0:T(8,128)(2,1)}, u32[]{:S(2)}, u32[]{:S(2)}) async-start(bf16[4,320,1024]{2,1,0:T(8,128)(2,1)} %param.29), calls=%async_computation.2 | async-start | bytes 5242880 | tf_op jit(solution)/shard_map/all_to_all | solution.py:143
  237.7 205.4 %reduce-scatter.10.cloned.1.call-start = ((), (), s32[]{:S(2)}) async-start(), calls=%async_computation.9 | async-start | bytes 5160960 | tf_op jit(solution)/shard_map/reduce_scatter | solution.py:295
  245.3 13.9 %copy-start.5 = (f32[4,320,1024]{2,1,0:T(8,128)}, f32[4,320,1024]{2,1,0:T(8,128)S(1)}, u32[]{:S(2)}) copy-start(f32[4,320,1024]{2,1,0:T(8,128)S(1)} %convert_element_type.149) | copy-start | bytes 15728644
  259.2 7.9 copy-start.2
  267.1 12.0 %collective-permute-start.1 = (bf16[1,640,64]{1,2,0:T(8,128)(2,1)S(1)}, bf16[1,640,64]{1,2,0:T(8,128)(2,1)S(1)}, u32[]{:S(2)}, u32[]{:S(2)}) collective-permute-start(bf16[1,640,64]{1,2,0:T(8,128)(2,1)S(1)} %get-tuple-element.40), channel_id=1, source_target_pairs={{0,4},{1,5},{2,6},{3,7},{8,12},{9,13},{10,14},{11,15},{16,20},{17,... | collective-permute-start | bytes 245768 | tf_op jit(solution)/shard_map/ppermute | solution.py:122
  277.7 10.6 %collective-permute-start.3 = (bf16[1,640,64]{1,2,0:T(8,128)(2,1)S(1)}, bf16[1,640,64]{1,2,0:T(8,128)(2,1)S(1)}, u32[]{:S(2)}, u32[]{:S(2)}) collective-permute-start(bf16[1,640,64]{1,2,0:T(8,128)(2,1)S(1)} %get-tuple-element.39), channel_id=1, source_target_pairs={{4,0},{5,1},{6,2},{7,3},{12,8},{13,9},{14,10},{15,11},{20,16},{21,... | collective-permute-start | bytes 245768 | tf_op jit(solution)/shard_map/ppermute | solution.py:123
  279.2 1.7 copy-start.3
  288.2 3.2 copy-start.6
  289.0 7.8 copy-start.7
  296.8 1.4 copy-start.11
  317.9 13.2 %collective-permute-start.4 = (bf16[1,640,64]{1,2,0:T(8,128)(2,1)S(1)}, bf16[1,640,64]{1,2,0:T(8,128)(2,1)S(1)}, u32[]{:S(2)}, u32[]{:S(2)}) collective-permute-start(bf16[1,640,64]{1,2,0:T(8,128)(2,1)S(1)} %get-tuple-element.38), channel_id=1, source_target_pairs={{4,0},{5,1},{6,2},{7,3},{12,8},{13,9},{14,10},{15,11},{20,16},{21,... | collective-permute-start | bytes 245768 | tf_op jit(solution)/shard_map/ppermute | solution.py:123
  319.2 12.9 %collective-permute-start.5 = (bf16[1,640,64]{1,2,0:T(8,128)(2,1)S(1)}, bf16[1,640,64]{1,2,0:T(8,128)(2,1)S(1)}, u32[]{:S(2)}, u32[]{:S(2)}) collective-permute-start(bf16[1,640,64]{1,2,0:T(8,128)(2,1)S(1)} %get-tuple-element.37), channel_id=1, source_target_pairs={{0,4},{1,5},{2,6},{3,7},{8,12},{9,13},{10,14},{11,15},{16,20},{17,... | collective-permute-start | bytes 245768 | tf_op jit(solution)/shard_map/ppermute | solution.py:122
  331.8 2.2 copy-start.9
  332.1 2.8 copy-start.4
  332.1 15.6 %slice-start = ((s8[5242880]{0:T(1024)(128)(4,1)}), s8[4194304]{0:T(1024)(128)(4,1)S(1)}, s32[]{:S(2)}) async-start(s8[5242880]{0:T(1024)(128)(4,1)} %bitcast.257), calls=%async_computation.15 | async-start | bytes 8388608
  334.9 12.8 %slice-start.1 = ((s8[5242880]{0:T(1024)(128)(4,1)}), s8[1048576]{0:T(1024)(128)(4,1)S(1)}, s32[]{:S(2)}) async-start(s8[5242880]{0:T(1024)(128)(4,1)} %bitcast.257), calls=%async_computation.16 | async-start | bytes 2097152
  347.7 17.4 %copy-start.14 = (bf16[1,640,1024]{1,2,0:T(8,128)(2,1)}, bf16[1,640,1024]{1,2,0:T(8,128)(2,1)S(1)}, u32[]{:S(2)}) copy-start(bf16[1,640,1024]{1,2,0:T(8,128)(2,1)S(1)} %get-tuple-element.35) | copy-start | bytes 3932164
  369.7 77.4 %reduce-scatter.12.cloned.1.call-start = ((), (), s32[]{:S(2)}) async-start(), calls=%async_computation.10 | async-start | bytes 4915200 | tf_op jit(solution)/shard_map/reduce_scatter | solution.py:295
  387.4 74.0 %reduce-scatter.16.cloned.1.call-start = ((), (), s32[]{:S(2)}) async-start(), calls=%async_computation.12 | async-start | bytes 12288000
  443.0 126.0 %all-reduce.4.cloned.1.call-start = ((), (), s32[]{:S(2)}) async-start(), calls=%async_computation.14 | async-start | bytes 5242880
  447.0 193.2 %reduce-scatter.14.cloned.1.call-start = ((), (), s32[]{:S(2)}) async-start(), calls=%async_computation.11 | async-start | bytes 2048000 | tf_op jit(solution)/shard_map/reduce_scatter | solution.py:296
  447.0 14.4 %copy-start.18 = (f32[4,320]{1,0:T(4,128)S(1)}, f32[4,320]{1,0:T(4,128)}, u32[]{:S(2)}) copy-start(f32[4,320]{1,0:T(4,128)} %get-tuple-element.48) | copy-start | bytes 15364
  447.1 14.5 %copy-start.8 = (bf16[1,640,1024]{1,2,0:T(8,128)(2,1)S(1)}, bf16[1,640,1024]{1,2,0:T(8,128)(2,1)}, u32[]{:S(2)}) copy-start(bf16[1,640,1024]{1,2,0:T(8,128)(2,1)} %get-tuple-element.36) | copy-start | bytes 3932164
  447.6 270.7 %reduce-scatter.18.cloned.1.call-start = ((), (), s32[]{:S(2)}) async-start(), calls=%async_computation.13 | async-start | bytes 5120000
  472.7 35.9 %all-to-all-start.1 = ((bf16[4,320,1024]{2,1,0:T(8,128)(2,1)}), bf16[4,320,1024]{2,1,0:T(8,128)(2,1)}, u32[]{:S(2)}, u32[]{:S(2)}) async-start(bf16[4,320,1024]{2,1,0:T(8,128)(2,1)} %bitcast.266), calls=%async_computation.1 | async-start | bytes 5242880 | tf_op jit(solution)/shard_map/all_to_all | solution.py:156
  508.6 4.9 copy-start.32
  508.6 35.4 %all-to-all-start.3 = ((bf16[4,320,1024]{2,1,0:T(8,128)(2,1)}), bf16[4,320,1024]{2,1,0:T(8,128)(2,1)}, u32[]{:S(2)}, u32[]{:S(2)}) async-start(bf16[4,320,1024]{2,1,0:T(8,128)(2,1)} %bitcast.265), calls=%async_computation.3 | async-start | bytes 5242880 | tf_op jit(solution)/shard_map/all_to_all | solution.py:156
  829.0 8.0 copy-start.1
  832.6 3.5 copy-start.10
  (3 other events, 2.8 us)
Sparse Core Ops, SparseCore 0:
  369.8 12.8 reduce-scatter.9
  387.5 12.6 reduce-scatter.11
  443.2 18.2 reduce-scatter.15
  463.6 105.3 all-reduce.3
  571.2 52.7 reduce-scatter.13
  626.3 91.9 reduce-scatter.17
where the time goes:
time: 856 us; the launch traced here: 844 us
  Pallas kernels  391 us (46%)
  local copies, waits for them, and re-layouts  138 us (16%)
  waiting for transfers between devices  111 us (13%)
  matrix products  99.3 us (12%)
  other arithmetic  55.9 us (7%)
  starting transfers between devices  32.6 us (4%)
  between operations  15.9 us (2%)
    pallas_call x13, Pallas kernels, exchange(): pl.pallas_call(functools.partial(_exchange_kernel, sizes, group, gather),...  391 us
    unnamed x9, waiting for transfers between devices  68.1 us
    unnamed x80, local copies, waits for them, and re-layouts  59.1 us
    all_to_all x2, waiting for transfers between devices, to_channels(): x = lax.all_to_all(x, 'ch', 0, 0, tiled=True)  43.1 us
    dot_general x1, matrix products, local(): jnp.einsum('dh,rhl->rdl', w_in, grad_inner, preferred_element_type=jnp.fl...  17.2 us
  transfers between devices with their start and end apart: 16, of which 5 were waited for; matrix products, arithmetic and copies ran while one was open for 23% of the time, Pallas kernels for 35%

commit v1 on v0

--- a/solution.py
+++ b/solution.py
@@ -19,7 +19,7 @@
 MESH_ID = pl.DeviceIdType.MESH
 
 
-def _exchange_kernel(sizes, group, gather, x_ref, o_ref, send_sem, recv_sem, own_sem):
+def _exchange_kernel(sizes, group, gather, x_ref, o_ref, send_sem, recv_sem):
     coords = {a: lax.axis_index(a) for a in MESH_AXES}
     me = 0
     for a in group:
@@ -51,9 +51,6 @@
         )
         copy.start()
         copies.append(copy)
-    own = pltpu.make_async_copy(x_ref if gather else x_ref.at[me], o_ref.at[me], own_sem)
-    own.start()
-    own.wait()
     for copy in copies:
         copy.wait()
 
@@ -65,7 +62,7 @@
         return x[None] if gather else x
     out_shape = (count,) + x.shape if gather else x.shape
     moved = x.size * x.dtype.itemsize * (count if gather else 1)
-    return pl.pallas_call(
+    out = pl.pallas_call(
         functools.partial(_exchange_kernel, sizes, group, gather),
         out_shape=jax.ShapeDtypeStruct(out_shape, x.dtype),
         in_specs=[pl.BlockSpec(memory_space=pl.ANY)],
@@ -73,11 +70,15 @@
         scratch_shapes=[
             pltpu.SemaphoreType.DMA((count - 1,)),
             pltpu.SemaphoreType.DMA((count - 1,)),
-            pltpu.SemaphoreType.DMA(()),
         ],
         compiler_params=pltpu.CompilerParams(collective_id=collective_id, has_side_effects=True),
         cost_estimate=pl.CostEstimate(flops=0, transcendentals=0, bytes_accessed=2 * moved),
     )(x)
+    me = 0
+    for a in group:
+        me = me * sizes[a] + lax.axis_index(a)
+    own = x if gather else lax.dynamic_index_in_dim(x, me, 0, keepdims=False)
+    return lax.dynamic_update_index_in_dim(out, own, me, 0)
 
 
 def gelu_exact(values):
@@ -205,15 +206,22 @@
         cut += n
     g0, s0, b_in, g1, s1, b_cv, g2, s2, b_out = full
     sidx = lax.axis_index("seq")
-    w_in = lax.dynamic_slice_in_dim(w_inner, sidx * (dloc // seqs), dloc // seqs, 0)
-    w_cv = lax.dynamic_slice_in_dim(w_conv, sidx * (hloc // seqs), hloc // seqs, 1)
-    w_out = lax.dynamic_slice_in_dim(w_outer, sidx * (hloc // seqs), hloc // seqs, 0)
-    w_in = exchange(exchange(w_in, ("ch",), 1, gather=True), ("seq",), 2, gather=True)
-    w_cv = exchange(exchange(w_cv, ("ch",), 3, gather=True), ("seq",), 4, gather=True)
-    w_out = exchange(exchange(w_out, ("ch",), 5, gather=True), ("seq",), 6, gather=True)
-    w_in = w_in.transpose(1, 0, 2, 3).reshape(dim, hid)
-    w_cv = w_cv.transpose(2, 1, 0, 3, 4).reshape(KERNEL_TAPS, hid, hid)
-    w_out = w_out.transpose(1, 0, 2, 3).reshape(hid, dim)
+    halves = [
+        lax.dynamic_slice_in_dim(w_inner, sidx * (dloc // seqs), dloc // seqs, 0),
+        lax.dynamic_slice_in_dim(w_conv, sidx * (hloc // seqs), hloc // seqs, 1),
+        lax.dynamic_slice_in_dim(w_outer, sidx * (hloc // seqs), hloc // seqs, 0),
+    ]
+    packed = jnp.concatenate([h.reshape(-1) for h in halves])
+    packed = exchange(packed.reshape(-1, 128), ("ch",), 1, gather=True)
+    packed = lax.all_gather(packed, "seq", axis=0, tiled=False).reshape(seqs, nch, -1)
+    cut = 0
+    parts = []
+    for h in halves:
+        parts.append(packed[:, :, cut : cut + h.size].reshape((seqs, nch) + h.shape))
+        cut += h.size
+    w_in = parts[0].transpose(1, 0, 2, 3).reshape(dim, hid)
+    w_cv = parts[1].transpose(2, 1, 0, 3, 4).reshape(KERNEL_TAPS, hid, hid)
+    w_out = parts[2].transpose(1, 0, 2, 3).reshape(hid, dim)
 
     x = to_positions(inputs, nch, q_count)
     cot = to_positions(cotangent, nch, q_count)
@@ -294,8 +302,10 @@
     def reduce_weight(g, split_dim, cid):
         g = lax.psum_scatter(g, "seq", scatter_dimension=split_dim, tiled=True)
         g = lax.psum_scatter(g, "batch", scatter_dimension=split_dim, tiled=True)
-        g = jnp.sum(exchange(g, ("ch",), cid), axis=0)
-        g = exchange(g, ("seq", "batch"), cid + 1, gather=True)
+        g = lax.psum_scatter(g, "ch", scatter_dimension=0, tiled=True)
+        spread = seqs * batches
+        g = jnp.broadcast_to(g, (spread,) + g.shape[1:])
+        g = lax.all_to_all(g, ("seq", "batch"), 0, 0, tiled=True)
         return jnp.moveaxis(g, 0, split_dim - 1)
 
     red_outer = reduce_weight(outer_plus, 2, 7)

time: 856 us -> 850 us (level)
  Pallas kernels: 391 us -> 72.2 us
  waiting for transfers between devices: 111 us -> 292 us
  blocking collectives: 0 us -> 109 us
  local copies, waits for them, and re-layouts: 138 us -> 165 us
    pallas_call x13 -> x2, Pallas kernels: 391 us -> 72.2 us  [exchange(): pl.pallas_call(functools.partial(_exchange_kernel, sizes, group, gather),...]
    all_to_all x0 -> x2, blocking collectives: none -> 109 us  [the longest x1 72.1 us: reduce_weight(): g = lax.all_to_all(g, ('seq', 'batch'), 0, 0, tiled=True)]
    unnamed x9 -> x16, waiting for transfers between devices: 68.1 us -> 161 us
    all_to_all x0 -> x2, waiting for transfers between devices: none -> 70.7 us  [reduce_weight(): g = lax.all_to_all(g, ('seq', 'batch'), 0, 0, tiled=True)]
    reduce_scatter x1, waiting for transfers between devices: 0.01 us -> 35.4 us  [reduce_weight(): g = lax.psum_scatter(g, 'batch', scatter_dimension=split_dim, tiled=True)]
    all_to_all x2 -> x1, waiting for transfers between devices: 43.1 us -> 15.7 us  [to_channels(): x = lax.all_to_all(x, 'ch', 0, 0, tiled=True)]
    reshape x0 -> x9, local copies, waits for them, and re-layouts: none -> 22.9 us  [the longest x5 15.4 us: local(): parts.append(packed[:, :, cut:cut + h.size].reshape((seqs, nch) + h.shape))]
    reduce_scatter x2, waiting for transfers between devices: 0.04 us -> 8.92 us  [reduce_weight(): g = lax.psum_scatter(g, 'seq', scatter_dimension=split_dim, tiled=True)]
  transfers between devices with their start and end apart: 16 -> 21, of which waited for: 5 -> 8; matrix products, arithmetic and copies ran while one was open for 23% -> 27% of each run, Pallas kernels for 35% -> 3%
where the time goes in v1:
time: 850 us; the launch traced here: 842 us
  waiting for transfers between devices  292 us (34%)
  local copies, waits for them, and re-layouts  165 us (19%)
  blocking collectives  109 us (13%)
  matrix products  103 us (12%)
  Pallas kernels  72.2 us (8%)
  other arithmetic  52.5 us (6%)
  starting transfers between devices  32.7 us (4%)
  between operations  15.9 us (2%)
    unnamed x16, waiting for transfers between devices  161 us
    pallas_call x2, Pallas kernels, exchange(): pl.pallas_call(functools.partial(_exchange_kernel, sizes, group, gather),...  72.2 us
    all_to_all x1, blocking collectives, reduce_weight(): g = lax.all_to_all(g, ('seq', 'batch'), 0, 0, tiled=True)  72.1 us
    all_to_all x2, waiting for transfers between devices, reduce_weight(): g = lax.all_to_all(g, ('seq', 'batch'), 0, 0, tiled=True)  70.7 us
    unnamed x82, local copies, waits for them, and re-layouts  54.8 us
    all_to_all x1, blocking collectives, to_channels(): x = lax.all_to_all(x, 'ch', 0, 0, tiled=True)  36.8 us
    reduce_scatter x1, waiting for transfers between devices, reduce_weight(): g = lax.psum_scatter(g, 'batch', scatter_dimension=split_dim, tiled=True)  35.4 us
    dot_general x1, matrix products, local(): jnp.einsum('dh,rhl->rdl', w_in, grad_inner, preferred_element_type=jnp.fl...  17.2 us
  transfers between devices with their start and end apart: 21, of which 8 were waited for; matrix products, arithmetic and copies ran while one was open for 27% of the time, Pallas kernels for 3%

profile of v1, /device:TPU:0, one launch (start us, length us, event | category | flops | bytes accessed | tf_op | source)
XLA Modules:
  0.0 841.5 jit_solution(2910504064957870366)
XLA Ops:
  11.3 44.8 %shard_map.255 = bf16[4,3600,128]{2,1,0:T(8,128)(2,1)} custom-call(bf16[3600,128]{1,0:T(8,128)(2,1)} %bitcast.291), custom_call_target="tpu_custom_call" | custom-call | bytes 7372800 | tf_op jit(solution)/shard_map/pallas_call | solution.py:65
  58.4 4.7 all-to-all-start
  67.8 27.4 %shard_map.254 = f32[4,1920]{1,0:T(4,128)} custom-call(f32[1920]{0:T(1024)} %concatenate.46.x_ref), custom_call_target="tpu_custom_call" | custom-call | bytes 61440 | tf_op jit(solution)/shard_map/pallas_call | solution.py:65
  100.5 4.6 all-to-all-start.2
  105.1 4.7 convert_element_type.149
  114.5 6.7 reshape.1438
  121.2 4.2 fusion.178
  129.2 17.2 %fusion.83 = (f32[1024]{0:T(1024)S(1)}, f32[1024,640]{1,0:T(8,128)S(1)}) fusion(f32[640]{0:T(1024)S(1)} %add.182, bf16[1280,640]{1,0:T(8,128)(2,1)S(1)} %bitcast.296, f32[1280]{0:T(1024)S(1)} %add.177, f32[1280]{0:T(1024)S(1)} %mul.436, f32[1024]{0:T(1024)S(1)} %add_rsqrt_fusion.2, f32[1,1280,1,1,1,1,1024]{6,1,5,4,3,2,0:T(8,128)} %bitcast.279, ...), kind=kOutput, calls=%fused_computation.160 | convolution fusion | flops 1769470976 | bytes 9527808 | tf_op jit(solution)/shard_map/dh,rdl->rhl/dot_general | solution.py:240
  147.0 7.3 multiply_convert_fusion.1
  157.8 6.0 copy.87
  163.7 5.3 slice.213
  170.3 5.5 reshape.1442
  175.8 4.6 copy.85
  186.6 7.8 copy.92
  196.2 7.3 constant_dynamic-update-slice_fusion.1
  206.6 5.5 fusion.85
  213.5 11.6 %fusion.60 = (f32[640]{0:T(1024)S(1)}, f32[1024]{0:T(1024)S(1)}, f32[1024]{0:T(1024)S(1)}, f32[640]{0:T(1024)S(1)}, f32[1,640,1024]{1,2,0:T(8,128)S(1)}) fusion(f32[1024]{0:T(1024)S(1)} %add_rsqrt_fusion, f32[1024]{0:T(1024)S(1)} %broadcast_multiply_fusion.4, f32[640]{0:T(1024)S(1)} %add.189, f32[1024,640]{1,0:T(8,128)S(1)} %get-tuple-element.94, ...), kind=kOutput, calls=%fused_computation.111 | convolution fusion | flops 1732113152 | bytes 9531904 | tf_op jit(solution)/shard_map/hd,rdl->rhl/dot_general | solution.py:254
  225.2 8.1 convert_reduce_fusion.1
  240.1 5.9 fusion.186
  250.0 11.8 %fusion.66 = (f32[640]{0:T(1024)S(1)}, f32[1024]{0:T(1024)S(1)}, f32[1024]{0:T(1024)S(1)}, f32[640]{0:T(1024)S(1)}, f32[1,640,1024]{1,2,0:T(8,128)S(1)}) fusion(f32[1024]{0:T(1024)S(1)} %add_rsqrt_fusion.1, f32[1024]{0:T(1024)S(1)} %broadcast_multiply_fusion.5, f32[640]{0:T(1024)S(1)} %add.182, f32[1024,640]{1,0:T(8,128)S(1)} %copy-done.4, ...), kind=kOutput, calls=%fused_computation.122 | convolution fusion | flops 4248695808 | bytes 15921664 | tf_op jit(solution)/shard_map/oc,rol->rcl/dot_general | solution.py:269
  263.3 17.2 %multiply_reduce_fusion = (f32[1280]{0:T(1024)S(1)}, f32[1024]{0:T(1024)S(1)}, f32[1024]{0:T(1024)S(1)}, f32[1280]{0:T(1024)S(1)}, f32[1,1280,1024]{1,2,0:T(8,128)}) fusion(f32[1,1280,1024]{1,2,0:T(8,128)S(1)} %bitcast.278, f32[1024]{0:T(1024)S(1)} %broadcast_multiply_fusion.8, f32[1024]{0:T(1024)S(1)} %add_rsqrt_fusion.2, f32[1280]{0:T(1024)S(1)} %mul.436, ...), kind=kOutput, calls=%fused_computation.39 | convolution fusion | flops 1785196032 | bytes 13471744 | tf_op jit(solution)/shard_map/dh,rhl->rdl/dot_general | solution.py:276
  281.0 4.0 pad_maximum_fusion
  285.8 17.1 %fusion.79 = f32[4,320,640]{2,1,0:T(8,128)} fusion(bf16[4,320,1024]{2,1,0:T(8,128)(2,1)} %all-to-all-done, f32[4,320]{1,0:T(4,128)S(1)} %copy-done.20, f32[4,320]{1,0:T(4,128)S(1)} %copy-done.18, f32[1024]{0:T(1024)S(1)} %add_rsqrt_fusion.2, f32[1024]{0:T(1024)S(1)} %broadcast_multiply_fusion.8, bf16[1,640,1024]{1,2,0:T(8,128)(2,1)} %copy-done.14), kind=kOutput, calls=%fused_computation.156 | convolution fusion | flops 1769472000 | bytes 7227392 | tf_op jit(solution)/shard_map/rdl,rhl->dh/dot_general | solution.py:275
  302.9 3.8 copy.96
  306.8 8.9 %reduce-scatter.19.cloned.1.call-done = f32[4,160,640]{2,1,0:T(8,128)} async-done(((f32[4,320,640]{2,1,0:T(8,128)}), f32[4,160,640]{2,1,0:T(8,128)}) %reduce-scatter.19.cloned.1.call-update) | async-done | bytes 1638416 | tf_op jit(solution)/shard_map/reduce_scatter | solution.py:303
  315.8 9.8 %copy.100 = bf16[1,3200,1024]{2,1,0:T(8,128)(2,1)} copy(bf16[1,3200,1024]{1,2,0:T(8,128)(2,1)} %copy-done.7) | data formatting | bytes 13107200 | tf_op jit(solution)/shard_map/concatenate | solution.py:136
  325.6 9.8 %convolution_bitcast_fusion = f32[4,5,160,640]{3,2,0,1:T(8,128)} fusion(bf16[5,4,160,1024]{3,2,1,0:T(8,128)(2,1)} %bitcast.289, bf16[1,640,1024]{1,2,0:T(8,128)(2,1)S(1)} %get-tuple-element.61), kind=kOutput, calls=%fused_computation.83 | convolution fusion | flops 4194304000 | bytes 16056320 | tf_op jit(solution)/shard_map/rkcil,rol->ckio/dot_general | solution.py:260
  335.3 14.7 %copy.111 = f32[4,5,160,640]{2,0,1,3:T(4,128)} copy(f32[4,5,160,640]{3,2,0,1:T(8,128)} %convolution_bitcast_fusion) | data formatting | bytes 16384000
  350.1 14.2 %reshape.1473 = f32[640,3200]{1,0:T(8,128)} reshape(f32[640,5,4,160]{3,2,1,0:T(4,128)} %bitcast.276) | data formatting | bytes 16384000
  366.1 57.8 %all-reduce.8.cloned.1.call-done = f32[4,162,640]{1,0,2:T(4,128)} async-done(((f32[4,162,640]{1,0,2:T(4,128)}), f32[4,162,640]{1,0,2:T(4,128)}) %all-reduce.8.cloned.1.call-update) | async-done | bytes 1658896
  426.2 35.4 %reduce-scatter.21.cloned.1.call-done = f32[4,40,640]{2,1,0:T(8,128)} async-done(((f32[4,160,640]{2,1,0:T(8,128)}), f32[4,40,640]{2,1,0:T(8,128)}) %reduce-scatter.21.cloned.1.call-update) | async-done | bytes 409616 | tf_op jit(solution)/shard_map/reduce_scatter | solution.py:304
  461.6 17.8 %reduce-scatter.23.cloned.1.call-done = f32[320,3200]{1,0:T(8,128)} async-done(((f32[640,3200]{1,0:T(8,128)}), f32[320,3200]{1,0:T(8,128)}) %reduce-scatter.23.cloned.1.call-update) | async-done | bytes 4096016
  479.6 6.7 fusion.15
  486.3 4.4 copy.88
  490.7 4.5 all-to-all-start.1
  495.2 5.0 copy.93
  500.2 8.0 add_convert_fusion
  508.2 4.5 copy.94
  512.8 15.7 %all-to-all-done.1 = bf16[4,320,1024]{2,1,0:T(8,128)(2,1)} async-done(((bf16[4,320,1024]{2,1,0:T(8,128)(2,1)}), bf16[4,320,1024]{2,1,0:T(8,128)(2,1)}, u32[]{:S(2)}, u32[]{:S(2)}) %all-to-all-start.1) | async-done | bytes 2621472 | tf_op jit(solution)/shard_map/all_to_all | solution.py:157
  528.5 36.8 %all_to_all.35 = bf16[4,320,1024]{2,1,0:T(8,128)(2,1)} all-to-all(bf16[4,320,1024]{2,1,0:T(8,128)(2,1)} %bitcast.286), channel_id=1, replica_groups=mesh['batch'=4,'seq'=2,'ch'=4] {'ch'}, dimensions={0} | all-to-all | bytes 5242880 | tf_op jit(solution)/shard_map/all_to_all | solution.py:157
  566.3 72.1 %all_to_all.36 = f32[8,162,160]{1,2,0:T(8,128)S(1)} all-to-all(f32[8,162,160]{1,2,0:T(8,128)S(1)} %broadcast_in_dim.106), channel_id=1, replica_groups=mesh['batch'=4,'seq'=2,'ch'=4] {'seq','batch'}, dimensions={0} | all-to-all | bytes 1658880 | tf_op jit(solution)/shard_map/all_to_all | solution.py:308
  640.3 3.5 all-to-all-start.5
  651.9 84.2 %all-reduce.10.cloned.1.call-done = f32[4,5,160,80]{3,2,0,1:T(8,128)} async-done(((f32[4,5,160,80]{3,2,0,1:T(8,128)}), f32[4,5,160,80]{3,2,0,1:T(8,128)}) %all-reduce.10.cloned.1.call-update) | async-done | bytes 1024016
  739.9 4.9 all-to-all-start.6
  748.0 70.7 %all-to-all-done.6 = f32[8,5,160,80]{3,2,1,0:T(8,128)} async-done(((f32[8,5,160,80]{3,2,1,0:T(8,128)}), f32[8,5,160,80]{3,2,1,0:T(8,128)}, u32[]{:S(2)}, u32[]{:S(2)}) %all-to-all-start.6) | async-done | bytes 2048032 | tf_op jit(solution)/shard_map/all_to_all | solution.py:308
  818.6 5.5 copy.102
  824.1 4.3 reshape.1464
  828.4 3.6 copy.134
  (198 shorter events, 79.8 us)
Async XLA Ops:
  7.2 2.8 copy-start.15
  7.2 107.3 %all-gather.2.cloned.1.call-start = ((), (), s32[]{:S(2)}) async-start(), calls=%async_computation.14 | async-start | bytes 11059200 | tf_op jit(solution)/shard_map/all_gather | solution.py:216
  58.3 8.8 %copy-start.21 = (f32[320]{0:T(512)S(1)}, f32[320]{0:T(512)}, u32[]{:S(2)}) copy-start(f32[320]{0:T(512)} %param.17) | copy-start | bytes 3844
  58.3 8.8 %copy-start.22 = (f32[320]{0:T(512)S(1)}, f32[320]{0:T(512)}, u32[]{:S(2)}) copy-start(f32[320]{0:T(512)} %param.18) | copy-start | bytes 3844
  58.3 8.8 %copy-start.23 = (f32[320]{0:T(512)S(1)}, f32[320]{0:T(512)}, u32[]{:S(2)}) copy-start(f32[320]{0:T(512)} %param.28) | copy-start | bytes 3844
  58.3 8.8 %copy-start.24 = (f32[160]{0:T(256)S(1)}, f32[160]{0:T(256)}, u32[]{:S(2)}) copy-start(f32[160]{0:T(256)} %param.20) | copy-start | bytes 1924
  58.3 8.8 %copy-start.25 = (f32[160]{0:T(256)S(1)}, f32[160]{0:T(256)}, u32[]{:S(2)}) copy-start(f32[160]{0:T(256)} %param.21) | copy-start | bytes 1924
  58.3 8.8 %copy-start.26 = (f32[160]{0:T(256)S(1)}, f32[160]{0:T(256)}, u32[]{:S(2)}) copy-start(f32[160]{0:T(256)} %param.22) | copy-start | bytes 1924
  58.3 8.8 %copy-start.27 = (f32[160]{0:T(256)S(1)}, f32[160]{0:T(256)}, u32[]{:S(2)}) copy-start(f32[160]{0:T(256)} %param.24) | copy-start | bytes 1924
  58.3 8.8 %copy-start.28 = (f32[160]{0:T(256)S(1)}, f32[160]{0:T(256)}, u32[]{:S(2)}) copy-start(f32[160]{0:T(256)} %param.25) | copy-start | bytes 1924
  58.4 8.8 %copy-start.29 = (f32[160]{0:T(256)S(1)}, f32[160]{0:T(256)}, u32[]{:S(2)}) copy-start(f32[160]{0:T(256)} %param.26) | copy-start | bytes 1924
  58.4 42.1 %all-to-all-start = ((bf16[4,320,1024]{2,1,0:T(8,128)(2,1)}), bf16[4,320,1024]{2,1,0:T(8,128)(2,1)}, u32[]{:S(2)}, u32[]{:S(2)}) async-start(bf16[4,320,1024]{2,1,0:T(8,128)(2,1)} %param.15), calls=%async_computation | async-start | bytes 5242880 | tf_op jit(solution)/shard_map/all_to_all | solution.py:144
  63.9 36.4 %collective-permute-start = (s32[1,64]{1,0:T(1,128)S(1)}, s32[1,64]{1,0:T(1,128)S(1)}, u32[]{:S(2)}, u32[]{:S(2)}) collective-permute-start(s32[1,64]{1,0:T(1,128)S(1)} %get-tuple-element.89), channel_id=1, source_target_pairs={{0,4},{1,5},{2,6},{3,7},{8,12},{9,13},{10,14},{11,15},{16,20},{17,... | collective-permute-start | bytes 776 | tf_op jit(solution)/shard_map/ppermute | solution.py:123
  65.7 34.6 %collective-permute-start.2 = (s32[1,64]{1,0:T(1,128)S(1)}, s32[1,64]{1,0:T(1,128)S(1)}, u32[]{:S(2)}, u32[]{:S(2)}) collective-permute-start(s32[1,64]{1,0:T(1,128)S(1)} %get-tuple-element.90), channel_id=1, source_target_pairs={{4,0},{5,1},{6,2},{7,3},{12,8},{13,9},{14,10},{15,11},{20,16},{21,... | collective-permute-start | bytes 776 | tf_op jit(solution)/shard_map/ppermute | solution.py:124
  100.5 55.1 %all-to-all-start.2 = ((bf16[4,320,1024]{2,1,0:T(8,128)(2,1)}), bf16[4,320,1024]{2,1,0:T(8,128)(2,1)}, u32[]{:S(2)}, u32[]{:S(2)}) async-start(bf16[4,320,1024]{2,1,0:T(8,128)(2,1)} %param.29), calls=%async_computation.2 | async-start | bytes 5242880 | tf_op jit(solution)/shard_map/all_to_all | solution.py:144
  105.1 197.8 %reduce-scatter.17.cloned.1.call-start = ((), (), s32[]{:S(2)}) async-start(), calls=%async_computation.15 | async-start | bytes 5160960 | tf_op jit(solution)/shard_map/reduce_scatter | solution.py:303
  129.2 17.2 %copy-start.12 = (bf16[2,4,160,640]{3,2,0,1:T(8,128)(2,1)}, bf16[2,4,160,640]{3,2,0,1:T(8,128)(2,1)S(1)}, u32[]{:S(2)}) copy-start(bf16[2,4,160,640]{3,2,0,1:T(8,128)(2,1)S(1)} %copy.107) | copy-start | bytes 4915204
  146.4 7.9 copy-start.2
  154.3 40.1 %collective-permute-start.1 = (bf16[1,640,64]{1,2,0:T(8,128)(2,1)S(1)}, bf16[1,640,64]{1,2,0:T(8,128)(2,1)S(1)}, u32[]{:S(2)}, u32[]{:S(2)}) collective-permute-start(bf16[1,640,64]{1,2,0:T(8,128)(2,1)S(1)} %get-tuple-element.70), channel_id=1, source_target_pairs={{0,4},{1,5},{2,6},{3,7},{8,12},{9,13},{10,14},{11,15},{16,20},{17,... | collective-permute-start | bytes 245768 | tf_op jit(solution)/shard_map/ppermute | solution.py:123
  169.0 34.5 %collective-permute-start.3 = (bf16[1,640,64]{1,2,0:T(8,128)(2,1)S(1)}, bf16[1,640,64]{1,2,0:T(8,128)(2,1)S(1)}, u32[]{:S(2)}, u32[]{:S(2)}) collective-permute-start(bf16[1,640,64]{1,2,0:T(8,128)(2,1)S(1)} %get-tuple-element.69), channel_id=1, source_target_pairs={{4,0},{5,1},{6,2},{7,3},{12,8},{13,9},{14,10},{15,11},{20,16},{21,... | collective-permute-start | bytes 245768 | tf_op jit(solution)/shard_map/ppermute | solution.py:124
  194.4 1.7 copy-start.3
  203.5 3.2 copy-start.5
  204.3 7.8 copy-start.7
  212.1 1.4 copy-start.11
  233.3 12.9 %collective-permute-start.4 = (bf16[1,640,64]{1,2,0:T(8,128)(2,1)S(1)}, bf16[1,640,64]{1,2,0:T(8,128)(2,1)S(1)}, u32[]{:S(2)}, u32[]{:S(2)}) collective-permute-start(bf16[1,640,64]{1,2,0:T(8,128)(2,1)S(1)} %get-tuple-element.68), channel_id=1, source_target_pairs={{4,0},{5,1},{6,2},{7,3},{12,8},{13,9},{14,10},{15,11},{20,16},{21,... | collective-permute-start | bytes 245768 | tf_op jit(solution)/shard_map/ppermute | solution.py:124
  234.6 12.6 %collective-permute-start.5 = (bf16[1,640,64]{1,2,0:T(8,128)(2,1)S(1)}, bf16[1,640,64]{1,2,0:T(8,128)(2,1)S(1)}, u32[]{:S(2)}, u32[]{:S(2)}) collective-permute-start(bf16[1,640,64]{1,2,0:T(8,128)(2,1)S(1)} %get-tuple-element.67), channel_id=1, source_target_pairs={{0,4},{1,5},{2,6},{3,7},{8,12},{9,13},{10,14},{11,15},{16,20},{17,... | collective-permute-start | bytes 245768 | tf_op jit(solution)/shard_map/ppermute | solution.py:123
  246.9 2.2 copy-start.10
  247.2 2.8 copy-start.4
  247.2 15.8 %slice-start = ((s8[5242880]{0:T(1024)(128)(4,1)}), s8[4194304]{0:T(1024)(128)(4,1)S(1)}, s32[]{:S(2)}) async-start(s8[5242880]{0:T(1024)(128)(4,1)} %bitcast.277), calls=%async_computation.24 | async-start | bytes 8388608
  250.0 13.1 %slice-start.1 = ((s8[5242880]{0:T(1024)(128)(4,1)}), s8[1048576]{0:T(1024)(128)(4,1)S(1)}, s32[]{:S(2)}) async-start(s8[5242880]{0:T(1024)(128)(4,1)} %bitcast.277), calls=%async_computation.25 | async-start | bytes 2097152
  261.8 1.4 copy-start.13
  263.0 17.4 %copy-start.14 = (bf16[1,640,1024]{1,2,0:T(8,128)(2,1)}, bf16[1,640,1024]{1,2,0:T(8,128)(2,1)S(1)}, u32[]{:S(2)}) copy-start(bf16[1,640,1024]{1,2,0:T(8,128)(2,1)S(1)} %get-tuple-element.63) | copy-start | bytes 3932164
  285.1 30.6 %reduce-scatter.19.cloned.1.call-start = ((), (), s32[]{:S(2)}) async-start(), calls=%async_computation.16 | async-start | bytes 4915200 | tf_op jit(solution)/shard_map/reduce_scatter | solution.py:303
  302.8 121.1 %all-reduce.8.cloned.1.call-start = ((), (), s32[]{:S(2)}) async-start(), calls=%async_computation.20 | async-start | bytes 5242880
  306.8 154.8 %reduce-scatter.21.cloned.1.call-start = ((), (), s32[]{:S(2)}) async-start(), calls=%async_computation.17 | async-start | bytes 2048000 | tf_op jit(solution)/shard_map/reduce_scatter | solution.py:304
  315.7 163.7 %reduce-scatter.23.cloned.1.call-start = ((), (), s32[]{:S(2)}) async-start(), calls=%async_computation.18 | async-start | bytes 12288000
  364.3 201.0 %reduce-scatter.27.cloned.1.call-start = ((), (), s32[]{:S(2)}) async-start(), calls=%async_computation.22 | async-start | bytes 819200
  426.1 53.4 %copy-start.16 = (f32[4,320]{1,0:T(4,128)S(1)}, f32[4,320]{1,0:T(4,128)}, u32[]{:S(2)}) copy-start(f32[4,320]{1,0:T(4,128)} %get-tuple-element.78) | copy-start | bytes 15364
  426.1 53.4 %copy-start.8 = (bf16[1,640,1024]{1,2,0:T(8,128)(2,1)S(1)}, bf16[1,640,1024]{1,2,0:T(8,128)(2,1)}, u32[]{:S(2)}) copy-start(bf16[1,640,1024]{1,2,0:T(8,128)(2,1)} %get-tuple-element.66) | copy-start | bytes 3932164
  426.1 212.3 %reduce-scatter.29.cloned.1.call-start = ((), (), s32[]{:S(2)}) async-start(), calls=%async_computation.23 | async-start | bytes 512000
  461.6 183.4 %reduce-scatter.25.cloned.1.call-start = ((), (), s32[]{:S(2)}) async-start(), calls=%async_computation.19 | async-start | bytes 5120000
  490.7 37.8 %all-to-all-start.1 = ((bf16[4,320,1024]{2,1,0:T(8,128)(2,1)}), bf16[4,320,1024]{2,1,0:T(8,128)(2,1)}, u32[]{:S(2)}, u32[]{:S(2)}) async-start(bf16[4,320,1024]{2,1,0:T(8,128)(2,1)} %bitcast.285), calls=%async_computation.1 | async-start | bytes 5242880 | tf_op jit(solution)/shard_map/all_to_all | solution.py:157
  640.3 97.5 %all-to-all-start.5 = ((f32[8,40,640]{2,1,0:T(8,128)}), f32[8,40,640]{2,1,0:T(8,128)S(1)}, u32[]{:S(2)}, u32[]{:S(2)}) async-start(f32[8,40,640]{2,1,0:T(8,128)} %broadcast_in_dim.108), calls=%async_computation.8 | async-start | bytes 1638400 | tf_op jit(solution)/shard_map/all_to_all | solution.py:308
  643.9 92.2 %all-reduce.10.cloned.1.call-start = ((), (), s32[]{:S(2)}) async-start(), calls=%async_computation.21 | async-start | bytes 3276800
  648.4 2.9 copy-start.30
  739.9 78.8 %all-to-all-start.6 = ((f32[8,5,160,80]{3,2,1,0:T(8,128)}), f32[8,5,160,80]{3,2,1,0:T(8,128)}, u32[]{:S(2)}, u32[]{:S(2)}) async-start(f32[8,5,160,80]{3,2,1,0:T(8,128)} %broadcast_in_dim.110), calls=%async_computation.9 | async-start | bytes 6553600 | tf_op jit(solution)/shard_map/all_to_all | solution.py:308
  828.4 3.6 copy-start.6
  828.4 6.0 copy-start.1
  (7 other events, 5.7 us)
Sparse Core Ops, SparseCore 0:
  58.4 19.4 all-gather.1
  285.2 12.9 reduce-scatter.16
  303.0 12.7 reduce-scatter.18
  318.6 105.2 all-reduce.7
  426.2 35.3 reduce-scatter.20
  463.7 15.6 reduce-scatter.22
  483.1 34.6 reduce-scatter.26
  520.8 25.8 reduce-scatter.28
  549.0 95.9 reduce-scatter.24
  651.4 84.6 all-reduce.9
